TPU v7x, 32 devices: a whole 2x2x4 slice. The times are simulated.
32 devices in a mesh: dp: 8 (over z, y), tensor: 4 (over x, core).
Axes of the slice: x: 2, y: 2, z: 4, core: 2. Of those that a mesh axis runs over, the one named last changes fastest.
Arguments:
- tokens: bfloat16 [512, 1536], P('dp'), may hold values from -6 to 6
- norm_gain: float32 [1536], replicated, may hold values from 0.1 to 1.9
- w_query: bfloat16 [1536, 1024], P(None, 'tensor'), may hold values from -0.15625 to 0.15625
- w_keyval: bfloat16 [1536, 256], replicated, may hold values from -0.15625 to 0.15625
- w_out: bfloat16 [1024, 1536], P('tensor'), may hold values from -0.5 to 0.5
- kv_pool: bfloat16 [4096, 128, 256], P(('dp', 'tensor')), may hold values from -256 to 256
- page_table: int32 [512, 8], P('dp', 'tensor'), may hold values from 0 to 127, as said below
- positions: int32 [512], P('dp'), may hold values from 0 to 8191
- assignment: int32 [512], P('dp'), may hold values from 0 to 511, as said below
Outputs:
- attn_out: bfloat16 [512, 1536], P('dp')
Inputs may be any that keep to these rules, and one draw needn't show every extreme that they name: `assignment`: the serving slot is the serving device's dp index times 64 plus a local slot; each serving slot is taken by exactly one request; the 64 requests of one device go to 8 distinct devices, exactly 8 to each. `page_table`: on each device the entries form a permutation of 0 to 127.
All inputs are finite; a program needn't handle non-finite values.
Results may differ from a plain program's by a relative error of at most 0.03.
Values may be sent and summed in bfloat16 or wider, within the bound.
A program may use at most 64 MiB of HBM per device.

v0:
```python
import jax
import jax.numpy as jnp
from jax import lax
from jax.sharding import PartitionSpec as P

masked_score = -1e30
norm_eps = 1e-06
rotary_base = 10000.0


def combined_all(array, axis, join):
    gathered = jax.tree.map(
        lambda a, kind: lax.all_gather(a.astype(kind), axis),
        array,
        (jnp.bfloat16, jnp.bfloat16, jnp.bfloat16),
    )

    def take(source):
        return jax.tree.map(
            lambda a, own: lax.dynamic_index_in_dim(a, source, 0, False).astype(own.dtype),
            gathered,
            array,
        )

    return lax.fori_loop(
        1, lax.axis_size(axis), lambda source, state: join(state, take(source)), take(0)
    )


def as_sent(array):

    def short(part):
        return part.astype(jnp.bfloat16) if part.dtype == jnp.float32 else part

    return jax.tree.map(short, array)


def rotate(values, where, width):
    half = width // 2
    freqs = rotary_base ** (-jnp.arange(half, dtype=jnp.float32) * 2.0 / width)
    angles = where.astype(jnp.float32)[..., None] * freqs
    cosine = jnp.cos(angles)
    sine = jnp.sin(angles)
    first = values[..., :half]
    second = values[..., half:]
    return jnp.concatenate(
        [first * cosine - second * sine, first * sine + second * cosine], axis=-1
    )


def combine_stats(first, second):
    peak = jnp.maximum(first[0], second[0])
    first_scale = jnp.exp(first[0] - peak)
    second_scale = jnp.exp(second[0] - peak)
    total = first[1] * first_scale + second[1] * second_scale
    summed = first[2] * first_scale[..., None] + second[2] * second_scale[..., None]
    return (peak, total, summed)


def local(tokens, norm_gain, w_query, w_keyval, w_out, kv_pool, page_table, positions, assignment):
    head_width = w_keyval.shape[1] // 2
    row_count = tokens.shape[0]
    group_size = lax.axis_size("tensor")
    data_size = lax.axis_size("dp")
    local_heads = w_query.shape[1] // head_width
    all_heads = local_heads * group_size
    capacity = max(2, row_count // data_size)
    slots_all = data_size * capacity
    scale = head_width ** (-0.5)
    here = lax.axis_index("tensor")
    floats = tokens.astype(jnp.float32)
    normed = (
        floats * lax.rsqrt(jnp.mean(floats * floats, axis=-1, keepdims=True) + norm_eps) * norm_gain
    ).astype(jnp.bfloat16)
    query = jnp.dot(normed, w_query, preferred_element_type=jnp.float32).reshape(
        row_count, local_heads, head_width
    )
    query = rotate(query, positions[:, None], head_width).astype(jnp.bfloat16)
    key_value = jnp.dot(normed, w_keyval, preferred_element_type=jnp.float32)
    new_key = rotate(key_value[:, :head_width], positions, head_width).astype(jnp.bfloat16)
    new_value = key_value[:, head_width:].astype(jnp.bfloat16)
    target = assignment // row_count
    local_slot = assignment % row_count
    hits = (target[:, None] == jnp.arange(data_size, dtype=jnp.int32)[None, :]).astype(jnp.int32)
    order_in = jnp.sum(jnp.cumsum(hits, axis=0) * hits, axis=1) - 1
    place = target * capacity + order_in

    def to_buffer(values):
        empty = jnp.zeros((slots_all,) + values.shape[1:], values.dtype)
        filled = empty.at[place].set(values)
        return filled.reshape((data_size, capacity) + values.shape[1:])

    def source_buffer(values):
        return values.reshape((slots_all,) + values.shape[2:])[place]

    tags = to_buffer(jnp.stack([positions, local_slot + 1], axis=1))
    tags = lax.all_to_all(tags, "dp", split_axis=0, concat_axis=0, tiled=True).reshape(slots_all, 2)
    served_slot = tags[:, 1] - 1
    scatter_slot = jnp.where(served_slot < 0, row_count, served_slot)
    gather_slot = jnp.maximum(served_slot, 0)

    def compact(values):
        empty = jnp.zeros((row_count,) + values.shape[1:], values.dtype)
        return empty.at[scatter_slot].set(values, mode="drop")

    def expand(values):
        return values[gather_slot].reshape((data_size, capacity) + values.shape[1:])

    current = compact(tags[:, 0])
    full_query = lax.all_gather(query, "tensor", axis=1, tiled=True)
    served_heads = lax.all_to_all(
        to_buffer(full_query), "dp", split_axis=0, concat_axis=0, tiled=True
    )
    served_heads = compact(served_heads.reshape(slots_all, all_heads, head_width))
    page_rows = page_table.shape[1]
    page_len = kv_pool.shape[1]
    window = page_rows * group_size * page_len
    page_entries = kv_pool[page_table].reshape(row_count, page_rows * page_len, 2 * head_width)
    scores = (
        jnp.einsum(
            "vto,vio->vti",
            served_heads,
            page_entries[..., :head_width],
            preferred_element_type=jnp.float32,
        )
        * scale
    )
    cycle_slot = here * page_rows * page_len + jnp.arange(page_rows * page_len, dtype=jnp.int32)
    offset = jnp.mod(cycle_slot[None, :] - current[:, None], window)
    valid = ((offset != 0) & (current[:, None] - window + offset >= 0))[:, None, :]
    peak = jnp.max(jnp.where(valid, scores, masked_score), axis=2)
    weight_tensors = jnp.where(valid, jnp.exp(scores - peak[..., None]), 0.0)
    total = jnp.sum(weight_tensors, axis=2)
    summed = jnp.einsum(
        "rbi,ril->rbl",
        weight_tensors.astype(jnp.bfloat16),
        page_entries[..., head_width:],
        preferred_element_type=jnp.float32,
    )
    merged = combined_all((peak, total, summed), "tensor", combine_stats)
    returned = (
        lax.all_to_all(as_sent(expand(merged[0])), "dp", split_axis=0, concat_axis=0, tiled=True),
        lax.all_to_all(as_sent(expand(merged[1])), "dp", split_axis=0, concat_axis=0, tiled=True),
        lax.all_to_all(as_sent(expand(merged[2])), "dp", split_axis=0, concat_axis=0, tiled=True),
    )
    own_stats = tuple(
        (
            lax.dynamic_slice_in_dim(source_buffer(member), here * local_heads, local_heads, 1)
            for member in returned
        )
    )
    cache_peak, cache_total, cache_summed = own_stats
    self_score = (
        jnp.einsum("rhd,rd->rh", query, new_key, preferred_element_type=jnp.float32) * scale
    )
    overall = jnp.maximum(cache_peak, self_score)
    keep = jnp.exp(cache_peak - overall)
    fresh = jnp.exp(self_score - overall)
    full_total = cache_total * keep + fresh
    fresh_low = fresh.astype(jnp.bfloat16).astype(jnp.float32)
    full_summed = (
        cache_summed * keep[..., None]
        + fresh_low[..., None] * new_value.astype(jnp.float32)[:, None, :]
    )
    attended = (
        (full_summed / full_total[..., None])
        .astype(jnp.bfloat16)
        .reshape(row_count, local_heads * head_width)
    )
    partial_out = jnp.dot(attended, w_out, preferred_element_type=jnp.float32)
    return lax.psum(partial_out.astype(jnp.bfloat16), "tensor")


def solution(mesh):
    return jax.shard_map(
        local,
        mesh=mesh,
        in_specs=(
            P("dp", None),
            P(),
            P(None, "tensor"),
            P(),
            P("tensor", None),
            P(("dp", "tensor"), None, None),
            P("dp", "tensor"),
            P("dp"),
            P("dp"),
        ),
        out_specs=P("dp", None),
        check_vma=False,
    )
```

profile of v0, /device:TPU:0, one launch (start us, length us, event | category | flops | bytes accessed | tf_op | source)
XLA Modules:
  0.0 160.3 jit_solution(12733547716529152877)
XLA Ops:
  6.5 0.7 fusion.43
  7.3 0.7 pad_add_fusion
  7.9 0.1 copy.66
  8.1 0.1 reduce_window_sum.11
  8.2 0.2 select_reduce_fusion.1
  8.4 0.8 scatter_custom_fusion
  9.2 0.7 copy.68
  9.9 7.3 %all-to-all-start = ((s32[8,8,2]{1,2,0:T(2,128)}), s32[8,8,2]{1,2,0:T(2,128)S(1)}, u32[]{:S(2)}, u32[]{:S(2)}) async-start(s32[8,8,2]{1,2,0:T(2,128)} %copy.68), calls=%async_computation | async-start | bytes 16384 | tf_op jit(solution)/shard_map/all_to_all | solution.py:97
  17.2 0.7 convert_element_type.152
  17.8 1.1 fusion.15
  18.9 0.7 compare_select_fusion
  19.6 0.1 copy.73
  19.7 0.1 reshape.222
  19.9 1.6 fusion.25
  21.4 1.6 fusion.27
  23.0 0.1 fusion.50
  23.2 0.2 subtract_convert_fusion.1
  23.5 0.1 pad_maximum_fusion
  23.6 0.2 fusion.32
  23.8 5.4 %all_gather.17 = bf16[64,8,128]{2,0,1:T(8,128)(2,1)S(1)} all-gather(bf16[64,2,128]{2,0,1:T(8,128)(2,1)S(1)} %pad_maximum_fusion), channel_id=1, replica_groups=mesh['dp'=8,'tensor'=4] {'tensor'}, dimensions={1}, use_global_device_ids=true | all-gather | bytes 163840 | tf_op jit(solution)/shard_map/all_gather | solution.py:110
  29.2 0.1 copy.72
  29.3 0.7 broadcast.188.clone
  30.0 6.9 %scatter_fusion = bf16[64,8,128]{2,1,0:T(8,128)(2,1)} fusion(bf16[64,8,128]{2,1,0:T(8,128)(2,1)} %broadcast.188.clone, s32[64]{0:T(128)S(1)} %compare_select_fusion.3, bf16[64,8,128]{2,1,0:T(8,128)(2,1)S(1)} %copy.72), kind=kCustom, calls=%fused_computation.9 | custom fusion | bytes 393472 | tf_op jit(solution)/shard_map/scatter | solution.py:90
  36.9 10.0 %gather_fusion = bf16[128,128,256]{2,1,0:T(8,128)(2,1)} fusion(bf16[128,128,256]{2,1,0:T(8,128)(2,1)} %param.16, s32[1024]{0:T(1024)S(1)} %pad_clamp_fusion.2), kind=kCustom, calls=%fused_computation | custom fusion | bytes 16777728 | tf_op jit(solution)/shard_map/gather | solution.py:118
  46.8 6.0 %all-to-all-start.1 = ((bf16[8,8,8,128]{3,2,1,0:T(8,128)(2,1)}), bf16[8,8,8,128]{3,2,1,0:T(8,128)(2,1)S(1)}, u32[]{:S(2)}, u32[]{:S(2)}) async-start(bf16[8,8,8,128]{3,2,1,0:T(8,128)(2,1)} %bitcast.9), calls=%async_computation.1 | async-start | bytes 262144 | tf_op jit(solution)/shard_map/all_to_all | solution.py:111
  52.9 0.8 scatter_custom_fusion.1
  53.7 0.1 fusion.24
  53.8 6.5 %all-to-all-done.1 = bf16[8,8,8,128]{3,2,1,0:T(8,128)(2,1)S(1)} async-done(((bf16[8,8,8,128]{3,2,1,0:T(8,128)(2,1)}), bf16[8,8,8,128]{3,2,1,0:T(8,128)(2,1)S(1)}, u32[]{:S(2)}, u32[]{:S(2)}) %all-to-all-start.1) | async-done | bytes 131104 | tf_op jit(solution)/shard_map/all_to_all | solution.py:111
  60.3 2.5 %scatter_fusion.1 = bf16[64,8,128]{2,1,0:T(8,128)(2,1)S(1)} fusion(bf16[64,8,128]{2,1,0:T(8,128)(2,1)S(1)} %broadcast.188, s32[64]{0:T(128)S(1)} %get-tuple-element.216, bf16[64,8,128]{2,1,0:T(8,128)(2,1)S(1)} %bitcast.88), kind=kCustom, calls=%fused_computation.10 | custom fusion | bytes 393472 | tf_op jit(solution)/shard_map/scatter | solution.py:104
  62.8 3.5 %select_reduce_fusion = (f32[64,8]{1,0:T(8,128)S(1)}, f32[64,8,256]{2,1,0:T(8,128)S(1)}) fusion(pred[64,256]{1,0:T(8,128)(4,1)S(1)} %fusion.24, bf16[64,8,128]{2,1,0:T(8,128)(2,1)S(1)} %scatter_fusion.1, bf16[64,256,256]{2,1,0:T(8,128)(2,1)} %bitcast.82), kind=kOutput, calls=%fused_computation.27 | convolution fusion | flops 33947136 | bytes 4868096 | tf_op jit(solution)/shard_map/vto,vio->vti/dot_general | solution.py:120
  66.3 2.9 %fusion.10 = bf16[64,8,128]{2,1,0:T(8,128)(2,1)S(1)} fusion(bf16[64,256,256]{2,1,0:T(8,128)(2,1)} %bitcast.83, f32[64,8,256]{2,1,0:T(8,128)S(1)} %get-tuple-element.221, f32[64,8]{1,0:T(8,128)S(1)} %get-tuple-element.220, pred[64,256]{1,0:T(8,128)(4,1)S(1)} %fusion.24), kind=kOutput, calls=%fused_computation.25 | convolution fusion | flops 34013184 | bytes 4868096 | tf_op jit(solution)/shard_map/rbi,ril->rbl/dot_general | solution.py:134
  69.2 0.3 fusion.14
  69.6 5.2 %all-gather.4 = bf16[4,64,8]{1,2,0:T(8,128)(2,1)S(1)} all-gather(bf16[1,64,8]{1,2,0:T(8,128)(2,1)S(1)} %copy.75), channel_id=3, replica_groups=mesh['dp'=8,'tensor'=4] {'tensor'}, dimensions={0}, use_global_device_ids=true | all-gather | bytes 5120 | tf_op jit(solution)/shard_map/all_gather | solution.py:13
  74.8 5.1 %all-gather.3 = bf16[4,64,8]{1,2,0:T(8,128)(2,1)S(1)} all-gather(bf16[1,64,8]{1,2,0:T(8,128)(2,1)S(1)} %copy.74), channel_id=2, replica_groups=mesh['dp'=8,'tensor'=4] {'tensor'}, dimensions={0}, use_global_device_ids=true | all-gather | bytes 5120 | tf_op jit(solution)/shard_map/all_gather | solution.py:13
  79.9 7.2 %all-gather.2 = bf16[256,8,128]{2,1,0:T(8,128)(2,1)S(1)} all-gather(bf16[64,8,128]{2,1,0:T(8,128)(2,1)S(1)} %fusion.10), channel_id=4, replica_groups=mesh['dp'=8,'tensor'=4] {'tensor'}, dimensions={0}, use_global_device_ids=true | all-gather | bytes 655360 | tf_op jit(solution)/shard_map/all_gather | solution.py:13
  87.2 1.5 while.19
  87.2 0.1 copy.114
  87.4 0.3 fusion.58
  87.7 0.1 copy.114
  87.9 0.3 fusion.58
  88.2 0.1 copy.114
  88.4 0.3 fusion.58
  88.7 0.1 copy.76
  88.8 1.2 gather_fusion.3
  90.0 3.3 %all-to-all-start.3 = ((bf16[8,8,8]{2,1,0:T(8,128)(2,1)}), bf16[8,8,8]{2,1,0:T(8,128)(2,1)S(1)}, u32[]{:S(2)}, u32[]{:S(2)}) async-start(bf16[8,8,8]{2,1,0:T(8,128)(2,1)} %bitcast.65), calls=%async_computation.3 | async-start | bytes 32768 | tf_op jit(solution)/shard_map/all_to_all | solution.py:142
  93.4 0.1 copy.80
  93.5 1.2 gather_fusion.5
  94.7 5.2 %all-to-all-done.3 = bf16[8,8,8]{2,1,0:T(8,128)(2,1)S(1)} async-done(((bf16[8,8,8]{2,1,0:T(8,128)(2,1)}), bf16[8,8,8]{2,1,0:T(8,128)(2,1)S(1)}, u32[]{:S(2)}, u32[]{:S(2)}) %all-to-all-start.3) | async-done | bytes 1056 | tf_op jit(solution)/shard_map/all_to_all | solution.py:142
  99.9 3.3 %all-to-all-start.4 = ((bf16[8,8,8]{2,1,0:T(8,128)(2,1)}), bf16[8,8,8]{2,1,0:T(8,128)(2,1)S(1)}, u32[]{:S(2)}, u32[]{:S(2)}) async-start(bf16[8,8,8]{2,1,0:T(8,128)(2,1)} %bitcast.64), calls=%async_computation.4 | async-start | bytes 32768 | tf_op jit(solution)/shard_map/all_to_all | solution.py:143
  103.3 1.3 gather_fusion.1
  104.6 0.6 gather_fusion.4
  105.2 4.5 %all-to-all-done.4 = bf16[8,8,8]{2,1,0:T(8,128)(2,1)S(1)} async-done(((bf16[8,8,8]{2,1,0:T(8,128)(2,1)}), bf16[8,8,8]{2,1,0:T(8,128)(2,1)S(1)}, u32[]{:S(2)}, u32[]{:S(2)}) %all-to-all-start.4) | async-done | bytes 1056 | tf_op jit(solution)/shard_map/all_to_all | solution.py:143
  109.7 3.4 %all-to-all-start.2 = ((bf16[8,8,8,128]{3,2,1,0:T(8,128)(2,1)}), bf16[8,8,8,128]{3,2,1,0:T(8,128)(2,1)S(1)}, u32[]{:S(2)}, u32[]{:S(2)}) async-start(bf16[8,8,8,128]{3,2,1,0:T(8,128)(2,1)} %bitcast.18), calls=%async_computation.2 | async-start | bytes 262144 | tf_op jit(solution)/shard_map/all_to_all | solution.py:144
  113.2 0.6 gather_fusion.6
  114.0 0.1 copy.90
  114.1 0.1 copy.82
  114.2 0.1 copy.78
  114.3 0.1 copy.79
  114.4 6.0 %all-to-all-done.2 = bf16[8,8,8,128]{3,2,1,0:T(8,128)(2,1)S(1)} async-done(((bf16[8,8,8,128]{3,2,1,0:T(8,128)(2,1)}), bf16[8,8,8,128]{3,2,1,0:T(8,128)(2,1)S(1)}, u32[]{:S(2)}, u32[]{:S(2)}) %all-to-all-start.2) | async-done | bytes 131104 | tf_op jit(solution)/shard_map/all_to_all | solution.py:144
  120.4 0.6 gather_fusion.2
  121.0 0.3 fusion.23
  121.3 0.9 convolution_convert_fusion
  122.3 29.6 %all-reduce.2.cloned.1.call-done = bf16[64,1536]{1,0:T(8,128)(2,1)} async-done(((bf16[64,1536]{1,0:T(8,128)(2,1)}), bf16[64,1536]{1,0:T(8,128)(2,1)}) %all-reduce.2.cloned.1.call-update) | async-done | bytes 196624 | tf_op jit(solution)/shard_map/psum | solution.py:171
  151.8 1.6 %copy.131 = bf16[64,1536]{1,0:T(8,128)(2,1)} copy(bf16[64,1536]{1,0:T(8,128)(2,1)} %all-reduce.2.cloned.1.call-done) | data formatting | bytes 393216
  (38 shorter events, 1.2 us)
Async XLA Ops:
  6.5 114.8 %copy-start = (bf16[256,1536]{1,0:T(8,128)(2,1)S(1)}, bf16[256,1536]{1,0:T(8,128)(2,1)}, u32[]{:S(2)}) copy-start(bf16[256,1536]{1,0:T(8,128)(2,1)} %param.15) | copy-start | bytes 2359300
  9.9 37.0 %all-to-all-start = ((s32[8,8,2]{1,2,0:T(2,128)}), s32[8,8,2]{1,2,0:T(2,128)S(1)}, u32[]{:S(2)}, u32[]{:S(2)}) async-start(s32[8,8,2]{1,2,0:T(2,128)} %copy.68), calls=%async_computation | async-start | bytes 16384 | tf_op jit(solution)/shard_map/all_to_all | solution.py:97
  46.8 13.5 %all-to-all-start.1 = ((bf16[8,8,8,128]{3,2,1,0:T(8,128)(2,1)}), bf16[8,8,8,128]{3,2,1,0:T(8,128)(2,1)S(1)}, u32[]{:S(2)}, u32[]{:S(2)}) async-start(bf16[8,8,8,128]{3,2,1,0:T(8,128)(2,1)} %bitcast.9), calls=%async_computation.1 | async-start | bytes 262144 | tf_op jit(solution)/shard_map/all_to_all | solution.py:111
  90.0 9.9 %all-to-all-start.3 = ((bf16[8,8,8]{2,1,0:T(8,128)(2,1)}), bf16[8,8,8]{2,1,0:T(8,128)(2,1)S(1)}, u32[]{:S(2)}, u32[]{:S(2)}) async-start(bf16[8,8,8]{2,1,0:T(8,128)(2,1)} %bitcast.65), calls=%async_computation.3 | async-start | bytes 32768 | tf_op jit(solution)/shard_map/all_to_all | solution.py:142
  99.9 9.9 %all-to-all-start.4 = ((bf16[8,8,8]{2,1,0:T(8,128)(2,1)}), bf16[8,8,8]{2,1,0:T(8,128)(2,1)S(1)}, u32[]{:S(2)}, u32[]{:S(2)}) async-start(bf16[8,8,8]{2,1,0:T(8,128)(2,1)} %bitcast.64), calls=%async_computation.4 | async-start | bytes 32768 | tf_op jit(solution)/shard_map/all_to_all | solution.py:143
  109.7 10.7 %all-to-all-start.2 = ((bf16[8,8,8,128]{3,2,1,0:T(8,128)(2,1)}), bf16[8,8,8,128]{3,2,1,0:T(8,128)(2,1)S(1)}, u32[]{:S(2)}, u32[]{:S(2)}) async-start(bf16[8,8,8,128]{3,2,1,0:T(8,128)(2,1)} %bitcast.18), calls=%async_computation.2 | async-start | bytes 262144 | tf_op jit(solution)/shard_map/all_to_all | solution.py:144
  113.1 38.7 %all-reduce.2.cloned.1.call-start = ((), (), s32[]{:S(2)}) async-start(), calls=%async_computation.5 | async-start | bytes 393216 | tf_op jit(solution)/shard_map/psum | solution.py:171
Sparse Core Ops, SparseCore 0:
  122.4 29.3 all-reduce.1
where the time goes:
time: 161 us; the launch traced here: 160 us
  waiting for transfers between devices  51.7 us (32%)
  local copies, waits for them, and re-layouts  31.7 us (20%)
  starting transfers between devices  23.4 us (15%)
  blocking collectives  23 us (14%)
  between operations  13.6 us (8%)
  matrix products  10.6 us (7%)
  other arithmetic  6.19 us (4%)
    psum x1, waiting for transfers between devices, local(): return lax.psum(partial_out.astype(jnp.bfloat16), 'tensor')  29.6 us
    all_gather x3, blocking collectives, combined_all(): lax.all_gather(a.astype(kind), axis)  17.6 us
    gather x1, local copies, waits for them, and re-layouts, local(): kv_pool[page_table].reshape(row_count, page_rows * page_len, 2 * head_width)  9.96 us
    scatter x2, local copies, waits for them, and re-layouts, to_buffer(): filled = empty.at[place].set(values)  7.66 us
    all_to_all x1, starting transfers between devices, local(): lax.all_to_all(tags, 'dp', split_axis=0, concat_axis=0, tiled=True)  7.28 us
    all_to_all x1, waiting for transfers between devices, local(): lax.all_to_all(to_buffer(full_query), 'dp', split_axis=0, concat_axis=0,...  6.47 us
    all_to_all x1, waiting for transfers between devices, local(): lax.all_to_all(as_sent(expand(merged[2])), 'dp', split_axis=0, concat_axi...  6.02 us
    all_to_all x1, starting transfers between devices, local(): lax.all_to_all(to_buffer(full_query), 'dp', split_axis=0, concat_axis=0,...  6 us
  transfers between devices with their start and end apart: 6, of which 5 were waited for; matrix products, arithmetic and copies ran while one was open for 19% of the time, Pallas kernels for 0%

commit v1 on v0

--- a/solution.py
+++ b/solution.py
@@ -6,6 +6,24 @@
 masked_score = -1e30
 norm_eps = 1e-06
 rotary_base = 10000.0
+
+
+def part_turns_by_axis(row_data, comm_axis, pos_dim, axis_k):
+    mixed_arr = lax.psum(1, comm_axis)
+    low, field_out = (mixed_arr, lax.axis_index(comm_axis))
+    z2 = row_data.shape[pos_dim] // low
+    long_array = jnp.roll(row_data, -field_out * z2, axis=pos_dim)
+    u_next = lax.slice_in_dim(long_array, 0, z2, axis=pos_dim)
+    dd = 1
+    store = [u_next]
+    while dd < low:
+        work_now = lax.slice_in_dim(long_array, dd * z2, (dd + 1) * z2, axis=pos_dim)
+        store.append(
+            lax.ppermute(work_now, comm_axis, perm=[(kk, (kk + dd) % low) for kk in range(low)])
+        )
+        dd += 1
+    outcome_arr = jnp.concatenate(store[::-1], axis=axis_k)
+    return jnp.roll(outcome_arr, (field_out + 1) * store[0].shape[axis_k], axis=axis_k)
 
 
 def combined_all(array, axis, join):
@@ -94,7 +112,7 @@
         return values.reshape((slots_all,) + values.shape[2:])[place]
 
     tags = to_buffer(jnp.stack([positions, local_slot + 1], axis=1))
-    tags = lax.all_to_all(tags, "dp", split_axis=0, concat_axis=0, tiled=True).reshape(slots_all, 2)
+    tags = part_turns_by_axis(tags, comm_axis="dp", pos_dim=0, axis_k=0).reshape(slots_all, 2)
     served_slot = tags[:, 1] - 1
     scatter_slot = jnp.where(served_slot < 0, row_count, served_slot)
     gather_slot = jnp.maximum(served_slot, 0)

time: 161 us -> 164 us (1.019)
  starting transfers between devices: 23.4 us -> 31.7 us
  waiting for transfers between devices: 51.7 us -> 47.4 us
    ppermute x0 -> x7, starting transfers between devices: none -> 16.2 us  [part_turns_by_axis(): lax.ppermute(work_now, comm_axis, perm=[(kk, (kk + dd) % low) for kk in r...]
    all_to_all x1 -> x0, starting transfers between devices: 7.28 us -> none  [local(): lax.all_to_all(tags, 'dp', split_axis=0, concat_axis=0, tiled=True)]
    all_to_all x1, waiting for transfers between devices: 6.47 us -> 0.01 us  [local(): lax.all_to_all(to_buffer(full_query), 'dp', split_axis=0, concat_axis=0,...]
    all_to_all x1, starting transfers between devices: 6 us -> 3.37 us  [local(): lax.all_to_all(to_buffer(full_query), 'dp', split_axis=0, concat_axis=0,...]
    ppermute x0 -> x7, waiting for transfers between devices: none -> 2.11 us  [part_turns_by_axis(): lax.ppermute(work_now, comm_axis, perm=[(kk, (kk + dd) % low) for kk in r...]
    all_to_all x1, starting transfers between devices: 3.34 us -> 5.43 us  [local(): lax.all_to_all(as_sent(expand(merged[0])), 'dp', split_axis=0, concat_axi...]
  transfers between devices with their start and end apart: 6 -> 12, of which waited for: 5 -> 5; matrix products, arithmetic and copies ran while one was open for 19% -> 18% of each run, Pallas kernels for 0% -> 0%
where the time goes in v1:
time: 164 us; the launch traced here: 163 us
  waiting for transfers between devices  47.4 us (29%)
  starting transfers between devices  31.7 us (19%)
  local copies, waits for them, and re-layouts  31.2 us (19%)
  blocking collectives  23 us (14%)
  between operations  13.7 us (8%)
  matrix products  10.6 us (6%)
  other arithmetic  5.56 us (3%)
    psum x1, waiting for transfers between devices, local(): return lax.psum(partial_out.astype(jnp.bfloat16), 'tensor')  29.6 us
    all_gather x3, blocking collectives, combined_all(): lax.all_gather(a.astype(kind), axis)  17.6 us
    ppermute x7, starting transfers between devices, part_turns_by_axis(): lax.ppermute(work_now, comm_axis, perm=[(kk, (kk + dd) % low) for kk in r...  16.2 us
    gather x1, local copies, waits for them, and re-layouts, local(): kv_pool[page_table].reshape(row_count, page_rows * page_len, 2 * head_width)  9.96 us
    scatter x2, local copies, waits for them, and re-layouts, to_buffer(): filled = empty.at[place].set(values)  7.66 us
    all_to_all x1, waiting for transfers between devices, local(): lax.all_to_all(as_sent(expand(merged[2])), 'dp', split_axis=0, concat_axi...  5.95 us
    all_to_all x1, starting transfers between devices, local(): lax.all_to_all(as_sent(expand(merged[0])), 'dp', split_axis=0, concat_axi...  5.43 us
    all_gather x1, blocking collectives, local(): full_query = lax.all_gather(query, 'tensor', axis=1, tiled=True)  5.43 us
  transfers between devices with their start and end apart: 12, of which 5 were waited for; matrix products, arithmetic and copies ran while one was open for 18% of the time, Pallas kernels for 0%

profile of v1, /device:TPU:0, one launch (start us, length us, event | category | flops | bytes accessed | tf_op | source)
XLA Modules:
  0.0 163.2 jit_solution(13503259166468704683)
XLA Ops:
  6.5 0.7 fusion.45
  7.3 0.7 compare_select_fusion
  8.0 0.1 copy.62
  8.1 0.1 reduce_window_sum.11
  8.2 0.2 select_reduce_fusion.1
  8.4 0.8 scatter_custom_fusion
  9.2 0.1 copy.80
  9.3 3.0 %collective-permute-start.6 = (s32[1,8,2]{1,0,2:T(1,128)S(1)}, s32[1,8,2]{1,0,2:T(1,128)S(1)}, u32[]{:S(2)}, u32[]{:S(2)}) collective-permute-start(s32[1,8,2]{1,0,2:T(1,128)S(1)} %get-tuple-element.214), channel_id=1, source_target_pairs={{0,4},{4,8},{8,12},{12,16},{16,20},{20,24},{24,28},{28,0},{1,5},{5... | collective-permute-start | bytes 200 | tf_op jit(solution)/shard_map/ppermute | solution.py:22
  12.4 1.6 collective-permute-start.5
  13.9 2.5 %collective-permute-start.4 = (s32[1,8,2]{1,0,2:T(1,128)S(1)}, s32[1,8,2]{1,0,2:T(1,128)S(1)}, u32[]{:S(2)}, u32[]{:S(2)}) collective-permute-start(s32[1,8,2]{1,0,2:T(1,128)S(1)} %get-tuple-element.216), channel_id=1, source_target_pairs={{0,12},{4,16},{8,20},{12,24},{16,28},{20,0},{24,4},{28,8},{1,13},{... | collective-permute-start | bytes 200 | tf_op jit(solution)/shard_map/ppermute | solution.py:22
  16.5 1.2 collective-permute-start.3
  17.7 2.6 %collective-permute-start.2 = (s32[1,8,2]{1,0,2:T(1,128)S(1)}, s32[1,8,2]{1,0,2:T(1,128)S(1)}, u32[]{:S(2)}, u32[]{:S(2)}) collective-permute-start(s32[1,8,2]{1,0,2:T(1,128)S(1)} %get-tuple-element.218), channel_id=1, source_target_pairs={{0,20},{4,24},{8,28},{12,0},{16,4},{20,8},{24,12},{28,16},{1,21},{... | collective-permute-start | bytes 200 | tf_op jit(solution)/shard_map/ppermute | solution.py:22
  20.4 0.7 convert_element_type.152
  21.0 1.1 fusion.15
  22.1 1.6 fusion.25
  23.7 1.6 fusion.27
  25.3 0.1 fusion.52
  25.4 0.2 subtract_convert_fusion.1
  25.7 5.4 %all_gather.17 = bf16[64,8,128]{2,0,1:T(8,128)(2,1)S(1)} all-gather(bf16[64,2,128]{2,0,1:T(8,128)(2,1)S(1)} %pad_maximum_fusion), channel_id=1, replica_groups=mesh['dp'=8,'tensor'=4] {'tensor'}, dimensions={1}, use_global_device_ids=true | all-gather | bytes 163840 | tf_op jit(solution)/shard_map/all_gather | solution.py:128
  31.2 0.1 copy.66
  31.3 0.7 broadcast.189.clone
  31.9 6.9 %scatter_fusion = bf16[64,8,128]{2,1,0:T(8,128)(2,1)} fusion(bf16[64,8,128]{2,1,0:T(8,128)(2,1)} %broadcast.189.clone, s32[64]{0:T(128)S(1)} %compare_select_fusion.3, bf16[64,8,128]{2,1,0:T(8,128)(2,1)S(1)} %copy.66), kind=kCustom, calls=%fused_computation.9 | custom fusion | bytes 393472 | tf_op jit(solution)/shard_map/scatter | solution.py:108
  38.8 3.4 %all-to-all-start = ((bf16[8,8,8,128]{3,2,1,0:T(8,128)(2,1)}), bf16[8,8,8,128]{3,2,1,0:T(8,128)(2,1)S(1)}, u32[]{:S(2)}, u32[]{:S(2)}) async-start(bf16[8,8,8,128]{3,2,1,0:T(8,128)(2,1)} %bitcast.9), calls=%async_computation | async-start | bytes 262144 | tf_op jit(solution)/shard_map/all_to_all | solution.py:129
  42.3 0.1 copy.67
  42.3 0.1 reshape.222
  42.6 0.2 fusion.32
  42.8 10.0 %gather_fusion = bf16[128,128,256]{2,1,0:T(8,128)(2,1)} fusion(bf16[128,128,256]{2,1,0:T(8,128)(2,1)} %param.18, s32[1024]{0:T(1024)S(1)} %pad_clamp_fusion.2), kind=kCustom, calls=%fused_computation | custom fusion | bytes 16777728 | tf_op jit(solution)/shard_map/gather | solution.py:136
  52.8 3.7 %collective-permute-start.1 = (s32[1,8,2]{1,0,2:T(1,128)S(1)}, s32[1,8,2]{1,0,2:T(1,128)S(1)}, u32[]{:S(2)}, u32[]{:S(2)}) collective-permute-start(s32[1,8,2]{1,0,2:T(1,128)S(1)} %get-tuple-element.219), channel_id=1, source_target_pairs={{0,24},{4,28},{8,0},{12,4},{16,8},{20,12},{24,16},{28,20},{1,25},{... | collective-permute-start | bytes 200 | tf_op jit(solution)/shard_map/ppermute | solution.py:22
  56.5 1.5 collective-permute-start
  58.0 2.1 %collective-permute-done = s32[1,8,2]{1,0,2:T(1,128)S(1)} collective-permute-done((s32[1,8,2]{1,0,2:T(1,128)S(1)}, s32[1,8,2]{1,0,2:T(1,128)S(1)}, u32[]{:S(2)}, u32[]{:S(2)}) %collective-permute-start) | collective-permute-done | bytes 96 | tf_op jit(solution)/shard_map/ppermute | solution.py:22
  60.2 0.8 scatter_custom_fusion.1
  61.0 0.1 fusion.24
  61.2 2.5 %scatter_fusion.1 = bf16[64,8,128]{2,1,0:T(8,128)(2,1)S(1)} fusion(bf16[64,8,128]{2,1,0:T(8,128)(2,1)S(1)} %broadcast.189, s32[64]{0:T(128)S(1)} %get-tuple-element.225, bf16[64,8,128]{2,1,0:T(8,128)(2,1)S(1)} %bitcast.87), kind=kCustom, calls=%fused_computation.10 | custom fusion | bytes 393472 | tf_op jit(solution)/shard_map/scatter | solution.py:122
  63.6 3.5 %select_reduce_fusion = (f32[64,8]{1,0:T(8,128)S(1)}, f32[64,8,256]{2,1,0:T(8,128)S(1)}) fusion(pred[64,256]{1,0:T(8,128)(4,1)S(1)} %fusion.24, bf16[64,8,128]{2,1,0:T(8,128)(2,1)S(1)} %scatter_fusion.1, bf16[64,256,256]{2,1,0:T(8,128)(2,1)} %bitcast.82), kind=kOutput, calls=%fused_computation.27 | convolution fusion | flops 33947136 | bytes 4868096 | tf_op jit(solution)/shard_map/vto,vio->vti/dot_general | solution.py:138
  67.1 2.9 %fusion.10 = bf16[64,8,128]{2,1,0:T(8,128)(2,1)S(1)} fusion(bf16[64,256,256]{2,1,0:T(8,128)(2,1)} %bitcast.83, f32[64,8,256]{2,1,0:T(8,128)S(1)} %get-tuple-element.230, f32[64,8]{1,0:T(8,128)S(1)} %get-tuple-element.229, pred[64,256]{1,0:T(8,128)(4,1)S(1)} %fusion.24), kind=kOutput, calls=%fused_computation.25 | convolution fusion | flops 34013184 | bytes 4868096 | tf_op jit(solution)/shard_map/rbi,ril->rbl/dot_general | solution.py:152
  70.0 0.3 fusion.14
  70.4 5.2 %all-gather.4 = bf16[4,64,8]{1,2,0:T(8,128)(2,1)S(1)} all-gather(bf16[1,64,8]{1,2,0:T(8,128)(2,1)S(1)} %copy.69), channel_id=3, replica_groups=mesh['dp'=8,'tensor'=4] {'tensor'}, dimensions={0}, use_global_device_ids=true | all-gather | bytes 5120 | tf_op jit(solution)/shard_map/all_gather | solution.py:31
  75.6 5.1 %all-gather.3 = bf16[4,64,8]{1,2,0:T(8,128)(2,1)S(1)} all-gather(bf16[1,64,8]{1,2,0:T(8,128)(2,1)S(1)} %copy.68), channel_id=2, replica_groups=mesh['dp'=8,'tensor'=4] {'tensor'}, dimensions={0}, use_global_device_ids=true | all-gather | bytes 5120 | tf_op jit(solution)/shard_map/all_gather | solution.py:31
  80.8 7.2 %all-gather.2 = bf16[256,8,128]{2,1,0:T(8,128)(2,1)S(1)} all-gather(bf16[64,8,128]{2,1,0:T(8,128)(2,1)S(1)} %fusion.10), channel_id=4, replica_groups=mesh['dp'=8,'tensor'=4] {'tensor'}, dimensions={0}, use_global_device_ids=true | all-gather | bytes 655360 | tf_op jit(solution)/shard_map/all_gather | solution.py:31
  88.0 1.5 while.19
  88.2 0.3 fusion.61
  88.7 0.3 fusion.61
  89.2 0.3 fusion.61
  89.5 0.1 copy.70
  89.6 1.2 gather_fusion.3
  90.8 5.4 %all-to-all-start.2 = ((bf16[8,8,8]{2,1,0:T(8,128)(2,1)}), bf16[8,8,8]{2,1,0:T(8,128)(2,1)S(1)}, u32[]{:S(2)}, u32[]{:S(2)}) async-start(bf16[8,8,8]{2,1,0:T(8,128)(2,1)} %bitcast.65), calls=%async_computation.2 | async-start | bytes 32768 | tf_op jit(solution)/shard_map/all_to_all | solution.py:160
  96.3 0.1 copy.74
  96.4 1.2 gather_fusion.5
  97.6 5.2 %all-to-all-done.2 = bf16[8,8,8]{2,1,0:T(8,128)(2,1)S(1)} async-done(((bf16[8,8,8]{2,1,0:T(8,128)(2,1)}), bf16[8,8,8]{2,1,0:T(8,128)(2,1)S(1)}, u32[]{:S(2)}, u32[]{:S(2)}) %all-to-all-start.2) | async-done | bytes 1056 | tf_op jit(solution)/shard_map/all_to_all | solution.py:160
  102.8 3.3 %all-to-all-start.3 = ((bf16[8,8,8]{2,1,0:T(8,128)(2,1)}), bf16[8,8,8]{2,1,0:T(8,128)(2,1)S(1)}, u32[]{:S(2)}, u32[]{:S(2)}) async-start(bf16[8,8,8]{2,1,0:T(8,128)(2,1)} %bitcast.64), calls=%async_computation.3 | async-start | bytes 32768 | tf_op jit(solution)/shard_map/all_to_all | solution.py:161
  106.3 1.3 gather_fusion.1
  107.6 0.6 gather_fusion.4
  108.2 4.5 %all-to-all-done.3 = bf16[8,8,8]{2,1,0:T(8,128)(2,1)S(1)} async-done(((bf16[8,8,8]{2,1,0:T(8,128)(2,1)}), bf16[8,8,8]{2,1,0:T(8,128)(2,1)S(1)}, u32[]{:S(2)}, u32[]{:S(2)}) %all-to-all-start.3) | async-done | bytes 1056 | tf_op jit(solution)/shard_map/all_to_all | solution.py:161
  112.7 3.4 %all-to-all-start.1 = ((bf16[8,8,8,128]{3,2,1,0:T(8,128)(2,1)}), bf16[8,8,8,128]{3,2,1,0:T(8,128)(2,1)S(1)}, u32[]{:S(2)}, u32[]{:S(2)}) async-start(bf16[8,8,8,128]{3,2,1,0:T(8,128)(2,1)} %bitcast.18), calls=%async_computation.1 | async-start | bytes 262144 | tf_op jit(solution)/shard_map/all_to_all | solution.py:162
  116.1 0.6 gather_fusion.6
  117.1 0.1 copy.76
  117.2 0.1 copy.72
  117.3 0.1 copy.73
  117.4 5.9 %all-to-all-done.1 = bf16[8,8,8,128]{3,2,1,0:T(8,128)(2,1)S(1)} async-done(((bf16[8,8,8,128]{3,2,1,0:T(8,128)(2,1)}), bf16[8,8,8,128]{3,2,1,0:T(8,128)(2,1)S(1)}, u32[]{:S(2)}, u32[]{:S(2)}) %all-to-all-start.1) | async-done | bytes 131104 | tf_op jit(solution)/shard_map/all_to_all | solution.py:162
  123.3 0.6 gather_fusion.2
  124.0 0.3 fusion.23
  124.3 0.9 convolution_convert_fusion
  125.2 29.6 %all-reduce.2.cloned.1.call-done = bf16[64,1536]{1,0:T(8,128)(2,1)} async-done(((bf16[64,1536]{1,0:T(8,128)(2,1)}), bf16[64,1536]{1,0:T(8,128)(2,1)}) %all-reduce.2.cloned.1.call-update) | async-done | bytes 196624 | tf_op jit(solution)/shard_map/psum | solution.py:189
  154.8 1.6 copy.134
  (53 shorter events, 1.8 us)
Async XLA Ops:
  6.5 117.7 %copy-start = (bf16[256,1536]{1,0:T(8,128)(2,1)S(1)}, bf16[256,1536]{1,0:T(8,128)(2,1)}, u32[]{:S(2)}) copy-start(bf16[256,1536]{1,0:T(8,128)(2,1)} %param.17) | copy-start | bytes 2359300
  9.3 43.4 %collective-permute-start.6 = (s32[1,8,2]{1,0,2:T(1,128)S(1)}, s32[1,8,2]{1,0,2:T(1,128)S(1)}, u32[]{:S(2)}, u32[]{:S(2)}) collective-permute-start(s32[1,8,2]{1,0,2:T(1,128)S(1)} %get-tuple-element.214), channel_id=1, source_target_pairs={{0,4},{4,8},{8,12},{12,16},{16,20},{20,24},{24,28},{28,0},{1,5},{5... | collective-permute-start | bytes 200 | tf_op jit(solution)/shard_map/ppermute | solution.py:22
  12.4 44.1 %collective-permute-start.5 = (s32[1,8,2]{1,0,2:T(1,128)S(1)}, s32[1,8,2]{1,0,2:T(1,128)S(1)}, u32[]{:S(2)}, u32[]{:S(2)}) collective-permute-start(s32[1,8,2]{1,0,2:T(1,128)S(1)} %get-tuple-element.215), channel_id=1, source_target_pairs={{0,8},{4,12},{8,16},{12,20},{16,24},{20,28},{24,0},{28,4},{1,9},{5... | collective-permute-start | bytes 200 | tf_op jit(solution)/shard_map/ppermute | solution.py:22
  13.9 44.0 %collective-permute-start.4 = (s32[1,8,2]{1,0,2:T(1,128)S(1)}, s32[1,8,2]{1,0,2:T(1,128)S(1)}, u32[]{:S(2)}, u32[]{:S(2)}) collective-permute-start(s32[1,8,2]{1,0,2:T(1,128)S(1)} %get-tuple-element.216), channel_id=1, source_target_pairs={{0,12},{4,16},{8,20},{12,24},{16,28},{20,0},{24,4},{28,8},{1,13},{... | collective-permute-start | bytes 200 | tf_op jit(solution)/shard_map/ppermute | solution.py:22
  16.5 41.5 %collective-permute-start.3 = (s32[1,8,2]{1,0,2:T(1,128)S(1)}, s32[1,8,2]{1,0,2:T(1,128)S(1)}, u32[]{:S(2)}, u32[]{:S(2)}) collective-permute-start(s32[1,8,2]{1,0,2:T(1,128)S(1)} %get-tuple-element.217), channel_id=1, source_target_pairs={{0,16},{4,20},{8,24},{12,28},{16,0},{20,4},{24,8},{28,12},{1,17},{... | collective-permute-start | bytes 200 | tf_op jit(solution)/shard_map/ppermute | solution.py:22
  17.7 40.2 %collective-permute-start.2 = (s32[1,8,2]{1,0,2:T(1,128)S(1)}, s32[1,8,2]{1,0,2:T(1,128)S(1)}, u32[]{:S(2)}, u32[]{:S(2)}) collective-permute-start(s32[1,8,2]{1,0,2:T(1,128)S(1)} %get-tuple-element.218), channel_id=1, source_target_pairs={{0,20},{4,24},{8,28},{12,0},{16,4},{20,8},{24,12},{28,16},{1,21},{... | collective-permute-start | bytes 200 | tf_op jit(solution)/shard_map/ppermute | solution.py:22
  38.8 22.3 %all-to-all-start = ((bf16[8,8,8,128]{3,2,1,0:T(8,128)(2,1)}), bf16[8,8,8,128]{3,2,1,0:T(8,128)(2,1)S(1)}, u32[]{:S(2)}, u32[]{:S(2)}) async-start(bf16[8,8,8,128]{3,2,1,0:T(8,128)(2,1)} %bitcast.9), calls=%async_computation | async-start | bytes 262144 | tf_op jit(solution)/shard_map/all_to_all | solution.py:129
  52.8 5.2 %collective-permute-start.1 = (s32[1,8,2]{1,0,2:T(1,128)S(1)}, s32[1,8,2]{1,0,2:T(1,128)S(1)}, u32[]{:S(2)}, u32[]{:S(2)}) collective-permute-start(s32[1,8,2]{1,0,2:T(1,128)S(1)} %get-tuple-element.219), channel_id=1, source_target_pairs={{0,24},{4,28},{8,0},{12,4},{16,8},{20,12},{24,16},{28,20},{1,25},{... | collective-permute-start | bytes 200 | tf_op jit(solution)/shard_map/ppermute | solution.py:22
  56.5 3.6 %collective-permute-start = (s32[1,8,2]{1,0,2:T(1,128)S(1)}, s32[1,8,2]{1,0,2:T(1,128)S(1)}, u32[]{:S(2)}, u32[]{:S(2)}) collective-permute-start(s32[1,8,2]{1,0,2:T(1,128)S(1)} %get-tuple-element.220), channel_id=1, source_target_pairs={{0,28},{4,0},{8,4},{12,8},{16,12},{20,16},{24,20},{28,24},{1,29},{... | collective-permute-start | bytes 200 | tf_op jit(solution)/shard_map/ppermute | solution.py:22
  90.8 12.0 %all-to-all-start.2 = ((bf16[8,8,8]{2,1,0:T(8,128)(2,1)}), bf16[8,8,8]{2,1,0:T(8,128)(2,1)S(1)}, u32[]{:S(2)}, u32[]{:S(2)}) async-start(bf16[8,8,8]{2,1,0:T(8,128)(2,1)} %bitcast.65), calls=%async_computation.2 | async-start | bytes 32768 | tf_op jit(solution)/shard_map/all_to_all | solution.py:160
  102.8 9.8 %all-to-all-start.3 = ((bf16[8,8,8]{2,1,0:T(8,128)(2,1)}), bf16[8,8,8]{2,1,0:T(8,128)(2,1)S(1)}, u32[]{:S(2)}, u32[]{:S(2)}) async-start(bf16[8,8,8]{2,1,0:T(8,128)(2,1)} %bitcast.64), calls=%async_computation.3 | async-start | bytes 32768 | tf_op jit(solution)/shard_map/all_to_all | solution.py:161
  112.7 10.7 %all-to-all-start.1 = ((bf16[8,8,8,128]{3,2,1,0:T(8,128)(2,1)}), bf16[8,8,8,128]{3,2,1,0:T(8,128)(2,1)S(1)}, u32[]{:S(2)}, u32[]{:S(2)}) async-start(bf16[8,8,8,128]{3,2,1,0:T(8,128)(2,1)} %bitcast.18), calls=%async_computation.1 | async-start | bytes 262144 | tf_op jit(solution)/shard_map/all_to_all | solution.py:162
  116.1 38.7 %all-reduce.2.cloned.1.call-start = ((), (), s32[]{:S(2)}) async-start(), calls=%async_computation.4 | async-start | bytes 393216 | tf_op jit(solution)/shard_map/psum | solution.py:189
Sparse Core Ops, SparseCore 0:
  125.3 29.3 all-reduce.1
